TPU v7x, 32 devices: a whole 2x2x4 slice. The times are simulated.
32 devices in a mesh: dp: 16 (over z, x, core), mp: 2 (over y).
Axes of the slice: x: 2, y: 2, z: 4, core: 2. Of those that a mesh axis runs over, the one named last changes fastest.
Arguments:
- frames_in: float32 [12288, 768], P(('dp', 'mp')), may hold values from -6 to 6
- frames_cot: float32 [12288, 768], P(('dp', 'mp')), may hold values from -6 to 6
- clip_ids: int32 [12288], replicated, may hold values from 0 to 16, never falling along the last dimension, each value on 1 to 768 neighbouring positions
- frame_mask: int32 [12288], replicated, may hold values 0 or 1
- norm_gain: float32 [2, 2, 768], replicated, may hold values from 0.25 to 1.75
- norm_bias: float32 [2, 2, 768], replicated, may hold values from -2 to 2
- qkv_weight: bfloat16 [2, 768, 3, 768], P(None, 'dp', None, 'mp'), as said below
- qv_bias: float32 [2, 2, 768], P(None, None, 'mp'), may hold values from -0.4 to 0.4
- proj_weight: bfloat16 [2, 768, 768], P(None, ('mp', 'dp')), may hold values from -4 to 4
- up_weight: bfloat16 [2, 768, 3072], P(None, 'dp', 'mp'), may hold values from -0.21875 to 0.21875
- up_bias: float32 [2, 3072], P(None, 'mp'), may hold values from -3 to 3
- down_weight: bfloat16 [2, 3072, 768], P(None, ('mp', 'dp')), may hold values from -0.109375 to 0.109375
- out_biases: float32 [2, 2, 768], replicated, may hold values from -2 to 2
Outputs:
- frames_out: float32 [12288, 768], P(('dp', 'mp'))
- frames_grad: float32 [12288, 768], P(('dp', 'mp'))
- grad_qkv: float32 [2, 768, 3, 768], P(None, 'dp', None, 'mp')
- grad_qv_bias: float32 [2, 2, 768], P(None, None, 'mp')
- grad_proj: float32 [2, 768, 768], P(None, ('mp', 'dp'))
- grad_up: float32 [2, 768, 3072], P(None, 'dp', 'mp')
- grad_up_bias: float32 [2, 3072], P(None, 'mp')
- grad_down: float32 [2, 3072, 768], P(None, ('mp', 'dp'))
- grad_gain: float32 [2, 2, 768], replicated
- grad_norm_bias: float32 [2, 2, 768], replicated
- grad_out_biases: float32 [2, 2, 768], replicated
Inputs may be any that keep to these rules, and one draw needn't show every extreme that they name: `clip_ids`: clip numbers never fall from one frame to the next; each clip holds 1 to 768 frames and one holds exactly 768. `qkv_weight`: projection weights for queries, keys and values.
All inputs are finite; a program needn't handle non-finite values.
Results may differ from a plain program's by a relative error of at most 0.013.
Values may be sent and summed in bfloat16 or wider, within the bound.
A program may use at most 320 MiB of HBM per device.

v0:
```python
import jax
import jax.numpy as jnp
from jax import lax
from jax.sharding import PartitionSpec as P

HD = 64
epsilon = 1e-05


def padded_2(block, sides, width):
    for axis, dim in sides:
        count = lax.axis_size(axis)
        forward = [(i, i + 1) for i in range(count - 1)]
        backward = [(target, source) for source, target in forward]
        low = lax.ppermute(
            lax.slice_in_dim(block, block.shape[dim] - width, None, axis=dim), axis, forward
        )
        high = lax.ppermute(lax.slice_in_dim(block, 0, width, axis=dim), axis, backward)
        block = jnp.concatenate([low, block, high], axis=dim)
    return block


def shifted(x, axis, by):
    size = lax.axis_size(axis)
    pairs = [(i, i + by) for i in range(size) if 0 <= i + by < size]
    return lax.ppermute(x, axis, pairs)


def norm_forward(values, gain_vec, bias_vec):
    row_mean = jnp.mean(values, axis=-1, keepdims=True)
    centred = values - row_mean
    inverse = lax.rsqrt(jnp.mean(centred * centred, axis=-1, keepdims=True) + epsilon)
    normed = centred * inverse
    return ((normed * gain_vec + bias_vec).astype(jnp.bfloat16), normed, inverse)


def norm_backward(grad_out, normed, inverse, gain_vec):
    scaled = grad_out * gain_vec
    projected = (
        scaled
        - jnp.mean(scaled, axis=-1, keepdims=True)
        - normed * jnp.mean(scaled * normed, axis=-1, keepdims=True)
    )
    return (inverse * projected, jnp.sum(grad_out * normed, axis=0), jnp.sum(grad_out, axis=0))


def gelu_value(preact):
    return 0.5 * preact * (1.0 + jax.scipy.special.erf(preact * 0.7071067811865476))


def gelu_slope(preact):
    return (
        0.5 * (1.0 + jax.scipy.special.erf(preact * 0.7071067811865476))
        + preact * jnp.exp(-0.5 * preact * preact) * 0.3989422804014327
    )


def padded(values, tok_span, fill):
    border = jnp.full((tok_span,) + values.shape[1:], fill, values.dtype)
    return jnp.concatenate([border, values, border], axis=0)


def block_mask(query_ids, block_start, key_ids, key_valid, tok_span):
    query_pos = block_start + jnp.arange(query_ids.shape[0], dtype=jnp.int32)
    key_pos = jnp.arange(key_ids.shape[0], dtype=jnp.int32)
    same_clip = query_ids[:, None] == key_ids[None, :]
    visible = (key_valid[None, :] == 1) | (key_pos[None, :] == query_pos[:, None] + tok_span)
    return same_clip & visible


def window_ids(clip_ids, frame_mask, tok_span):
    offset = lax.axis_index("dp") * tok_span
    ids_pad = padded(clip_ids, tok_span, -1)
    valid_pad = padded(frame_mask, tok_span, 0)
    return (
        lax.dynamic_slice_in_dim(ids_pad, offset + tok_span, tok_span, 0),
        lax.dynamic_slice_in_dim(ids_pad, offset, 3 * tok_span, 0),
        lax.dynamic_slice_in_dim(valid_pad, offset, 3 * tok_span, 0),
    )


def fetch_weights(qkv_weight, proj_weight, up_weight, down_weight, depth):
    return (
        lax.all_gather(qkv_weight[depth], "dp", axis=0, tiled=True),
        lax.all_gather(proj_weight[depth], "dp", axis=0, tiled=True),
        lax.all_gather(up_weight[depth], "dp", axis=0, tiled=True),
        lax.all_gather(down_weight[depth], "dp", axis=0, tiled=True),
    )


def gather_rows(values):
    return lax.all_gather(values, "mp", axis=0, tiled=True)


def sum_rows(left, right):
    return lax.psum_scatter(
        jnp.dot(left, right, preferred_element_type=jnp.float32),
        "mp",
        scatter_dimension=0,
        tiled=True,
    )


def block_scores(query, keys, query_ids, key_ids, key_valid, offset):
    tok_span = query.shape[0]
    allowed = block_mask(query_ids, offset, key_ids, key_valid, tok_span)
    scores = jnp.einsum("qhd,khd->hqk", query, keys, preferred_element_type=jnp.float32) * HD ** (
        -0.5
    )
    return (query, jnp.where(allowed[None], scores, -1e30))


def attend(query, key_vals, query_ids, key_ids, key_valid):
    tok_span = query.shape[0]
    n_blocks = (tok_span + 1023) // 1024
    block_rows = tok_span // n_blocks
    keys = key_vals[:, 0]
    values = key_vals[:, 1]

    def one_block(block_id):
        offset = block_id * block_rows
        query_block, scores = block_scores(query, keys, query_ids, key_ids, key_valid, offset)
        row_max = jnp.max(scores, axis=-1, keepdims=True)
        log_total = row_max + jnp.log(jnp.sum(jnp.exp(scores - row_max), axis=-1, keepdims=True))
        prob_low = jnp.exp(scores - log_total).astype(jnp.bfloat16)
        attended = jnp.einsum(
            "hqk,khd->qhd", prob_low, values, preferred_element_type=jnp.float32
        ).astype(jnp.bfloat16)
        return (attended, log_total[..., 0])

    attended, log_totals = lax.map(one_block, jnp.arange(n_blocks, dtype=jnp.int32))
    return (attended.reshape(query.shape), log_totals)


def attend_back(query, key_vals, attended, grad_attn, log_totals, query_ids, key_ids, key_valid):
    tok_span = query.shape[0]
    n_blocks = (tok_span + 1023) // 1024
    block_rows = tok_span // n_blocks
    score_scale = HD ** (-0.5)
    keys = key_vals[:, 0]
    values = key_vals[:, 1]

    def one_block(key_grads, block_id):
        offset = block_id * block_rows
        query_block, scores = block_scores(query, keys, query_ids, key_ids, key_valid, offset)
        prob_full = jnp.exp(scores - log_totals[block_id][..., None])
        prob_low = prob_full.astype(jnp.bfloat16)
        grad_prob = jnp.einsum(
            "qhd,khd->hqk", grad_attn, values, preferred_element_type=jnp.float32
        )
        delta_row = jnp.sum(grad_attn.astype(jnp.float32) * attended.astype(jnp.float32), axis=-1).T
        score_low = (prob_full * (grad_prob - delta_row[..., None])).astype(jnp.bfloat16)
        grad_query = (
            jnp.einsum("hqk,khd->qhd", score_low, keys, preferred_element_type=jnp.float32)
            * score_scale
        )
        grad_key = (
            jnp.einsum("hqk,qhd->khd", score_low, query_block, preferred_element_type=jnp.float32)
            * score_scale
        )
        grad_value = jnp.einsum(
            "hqk,qhd->khd", prob_low, grad_attn, preferred_element_type=jnp.float32
        )
        return (key_grads + jnp.stack([grad_key, grad_value], axis=1), grad_query)

    start = jnp.zeros((3 * tok_span, 2) + query.shape[1:], jnp.float32)
    key_grads, grad_query = lax.scan(one_block, start, jnp.arange(n_blocks, dtype=jnp.int32))
    return (grad_query.reshape(query.shape), key_grads)


def widen(piece, full_width, mp_index):
    out_shape = piece.shape[:-1] + (full_width,)
    return lax.dynamic_update_slice_in_dim(
        jnp.zeros(out_shape, jnp.float32), piece, mp_index * piece.shape[-1], piece.ndim - 1
    )


def layer_forward(
    state, matrices, gain_pair, bias_pair, qv_pair, up_vec, out_pair, query_ids, key_ids, key_valid
):
    qkv_mat, proj_mat, up_mat, down_mat = matrices
    head_cols = qkv_mat.shape[-1]
    first_norm, hat_one, inv_one = norm_forward(state, gain_pair[0], bias_pair[0])
    first_full = gather_rows(first_norm)
    tok_span = first_full.shape[0]
    bias_three = jnp.stack([qv_pair[0], jnp.zeros_like(qv_pair[0]), qv_pair[1]])
    qkv_proj = jnp.dot(
        first_full,
        qkv_mat.reshape(qkv_mat.shape[0], 3 * head_cols),
        preferred_element_type=jnp.float32,
    )
    qkv_proj = (qkv_proj.reshape(tok_span, 3, head_cols) + bias_three).astype(jnp.bfloat16)
    query = qkv_proj[:, 0].reshape(tok_span, head_cols // HD, HD)
    key_vals = qkv_proj[:, 1:].reshape(tok_span, 2 * head_cols)
    key_vals = padded_2(key_vals, (("dp", 0),), tok_span)
    key_vals = key_vals.reshape(3 * tok_span, 2, head_cols // HD, HD)
    attended, log_totals = attend(query, key_vals, query_ids, key_ids, key_valid)
    attn_flat = attended.reshape(tok_span, head_cols)
    middle = state + sum_rows(attn_flat, proj_mat) + out_pair[0]
    second_norm, hat_two, inv_two = norm_forward(middle, gain_pair[1], bias_pair[1])
    second_full = gather_rows(second_norm)
    preact = jnp.dot(second_full, up_mat, preferred_element_type=jnp.float32) + up_vec
    hidden = gelu_value(preact).astype(jnp.bfloat16)
    result = middle + sum_rows(hidden, down_mat) + out_pair[1]
    stored = {
        "hat_one": hat_one,
        "inv_one": inv_one,
        "first_full": first_full,
        "query": query,
        "key_vals": key_vals,
        "attended": attended,
        "log_totals": log_totals,
        "hat_two": hat_two,
        "inv_two": inv_two,
        "second_full": second_full,
        "preact": preact,
        "hidden": hidden,
    }
    return (stored, result)


def layer_backward(gradient, stored, matrices, gain_pair, query_ids, key_ids, key_valid):
    qkv_mat, proj_mat, up_mat, down_mat = matrices
    head_cols = qkv_mat.shape[-1]
    grad_full = gather_rows(gradient.astype(jnp.bfloat16))
    grad_down = jnp.dot(stored["hidden"].T, grad_full, preferred_element_type=jnp.float32)
    grad_pre = jnp.dot(grad_full, down_mat.T, preferred_element_type=jnp.float32) * gelu_slope(
        stored["preact"]
    )
    grad_upb = jnp.sum(grad_pre, axis=0)
    pre_low = grad_pre.astype(jnp.bfloat16)
    grad_up = jnp.dot(stored["second_full"].T, pre_low, preferred_element_type=jnp.float32)
    grad_second = sum_rows(pre_low, up_mat.T)
    back_two, gain_two, shift_two = norm_backward(
        grad_second, stored["hat_two"], stored["inv_two"], gain_pair[1]
    )
    grad_middle = gradient + back_two
    middle_full = gather_rows(grad_middle.astype(jnp.bfloat16))
    attended = stored["attended"]
    tok_span = attended.shape[0]
    grad_proj = jnp.dot(
        attended.reshape(tok_span, head_cols).T, middle_full, preferred_element_type=jnp.float32
    )
    grad_attn = jnp.dot(middle_full, proj_mat.T, preferred_element_type=jnp.float32).astype(
        jnp.bfloat16
    )
    grad_attn = grad_attn.reshape(attended.shape)
    grad_query, key_grads = attend_back(
        stored["query"],
        stored["key_vals"],
        attended,
        grad_attn,
        stored["log_totals"],
        query_ids,
        key_ids,
        key_valid,
    )
    key_grads = key_grads.reshape(3 * tok_span, 2 * head_cols)
    own_grads = key_grads[tok_span : 2 * tok_span]
    for step_by, piece in ((1, key_grads[2 * tok_span :]), (-1, key_grads[:tok_span])):
        own_grads = own_grads + shifted(piece.astype(jnp.bfloat16), "dp", step_by).astype(
            piece.dtype
        )
    grad_query = grad_query.reshape(tok_span, head_cols)
    grad_key = own_grads[:, :head_cols]
    grad_value = own_grads[:, head_cols:]
    grad_qv = jnp.stack([jnp.sum(grad_query, axis=0), jnp.sum(grad_value, axis=0)])
    qkv_low = (
        jnp.stack([grad_query, grad_key, grad_value], axis=1)
        .astype(jnp.bfloat16)
        .reshape(tok_span, 3 * head_cols)
    )
    grad_qkv = jnp.dot(stored["first_full"].T, qkv_low, preferred_element_type=jnp.float32).reshape(
        -1, 3, head_cols
    )
    grad_first = sum_rows(qkv_low, qkv_mat.reshape(-1, 3 * head_cols).T)
    back_one, gain_one, shift_one = norm_backward(
        grad_first, stored["hat_one"], stored["inv_one"], gain_pair[0]
    )
    new_grad = grad_middle + back_one
    mp_index = lax.axis_index("mp")
    mp_count = lax.axis_size("mp")
    small = (
        jnp.stack([gain_one, gain_two]),
        jnp.stack([shift_one, shift_two]),
        jnp.stack([jnp.sum(grad_middle, axis=0), jnp.sum(gradient, axis=0)]),
        widen(grad_qv, head_cols * mp_count, mp_index),
        widen(grad_upb, grad_upb.shape[0] * mp_count, mp_index),
    )
    return (new_grad, (grad_qkv, grad_proj, grad_up, grad_down), small)


def body(
    frames_in,
    frames_cot,
    clip_ids,
    frame_mask,
    norm_gain,
    norm_bias,
    qkv_weight,
    qv_bias,
    proj_weight,
    up_weight,
    up_bias,
    down_weight,
    out_biases,
):
    layers = qkv_weight.shape[0]
    tok_span = frames_in.shape[0] * lax.axis_size("mp")
    query_ids, key_ids, key_valid = window_ids(clip_ids, frame_mask, tok_span)
    stored_all = []
    state = frames_in
    for depth in range(layers):
        matrices = fetch_weights(qkv_weight, proj_weight, up_weight, down_weight, depth)
        stored, state = layer_forward(
            state,
            matrices,
            norm_gain[depth],
            norm_bias[depth],
            qv_bias[depth],
            up_bias[depth],
            out_biases[depth],
            query_ids,
            key_ids,
            key_valid,
        )
        stored_all.append(stored)
    gradient = frames_cot
    weight_grads = []
    small_grads = []
    for depth in range(layers - 1, -1, -1):
        matrices = fetch_weights(qkv_weight, proj_weight, up_weight, down_weight, depth)
        gradient, mats_grad, small = layer_backward(
            gradient, stored_all[depth], matrices, norm_gain[depth], query_ids, key_ids, key_valid
        )
        mats_grad = (
            lax.psum_scatter(mats_grad[0], "dp", scatter_dimension=0, tiled=True),
            lax.psum_scatter(mats_grad[1], "dp", scatter_dimension=0, tiled=True),
            lax.psum_scatter(mats_grad[2], "dp", scatter_dimension=0, tiled=True),
            lax.psum_scatter(mats_grad[3], "dp", scatter_dimension=0, tiled=True),
        )
        small = lax.psum((small[0], small[1], small[2], small[3], small[4]), ("dp", "mp"))
        weight_grads.insert(0, mats_grad)
        small_grads.insert(0, small)
    stacked_w = tuple((jnp.stack([entry[slot] for entry in weight_grads]) for slot in range(4)))
    stacked_s = tuple((jnp.stack([entry[slot] for entry in small_grads]) for slot in range(5)))
    mp_index = lax.axis_index("mp")
    head_cols = qv_bias.shape[-1]
    up_cols = up_bias.shape[-1]
    grad_qv = lax.dynamic_slice_in_dim(stacked_s[3], mp_index * head_cols, head_cols, 2)
    grad_upb = lax.dynamic_slice_in_dim(stacked_s[4], mp_index * up_cols, up_cols, 1)
    return (
        state,
        gradient,
        stacked_w[0],
        grad_qv,
        stacked_w[1],
        stacked_w[2],
        grad_upb,
        stacked_w[3],
        stacked_s[0],
        stacked_s[1],
        stacked_s[2],
    )


def solution(mesh):
    placed = (
        P(("dp", "mp"), None),
        P(("dp", "mp"), None),
        P(),
        P(),
        P(),
        P(),
        P(None, "dp", None, "mp"),
        P(None, None, "mp"),
        P(None, ("mp", "dp"), None),
        P(None, "dp", "mp"),
        P(None, "mp"),
        P(None, ("mp", "dp"), None),
        P(),
    )
    return jax.shard_map(
        body,
        mesh=mesh,
        in_specs=placed,
        out_specs=(
            P(("dp", "mp"), None),
            P(("dp", "mp"), None),
            P(None, "dp", None, "mp"),
            P(None, None, "mp"),
            P(None, ("mp", "dp"), None),
            P(None, "dp", "mp"),
            P(None, "mp"),
            P(None, ("mp", "dp"), None),
            P(),
            P(),
            P(),
        ),
        check_vma=False,
    )
```

profile of v0, /device:TPU:0, one launch (start us, length us, event | category | flops | bytes accessed | tf_op | source)
XLA Modules:
  0.0 1947.3 jit_solution(16931985044161411071)
XLA Ops:
  14.8 39.2 %all-gather.39.cloned.1.call-done = bf16[1,768,3,384]{3,1,2,0:T(8,128)(2,1)} async-done(((bf16[1,48,3,384]{3,1,2,0:T(8,128)(2,1)}), bf16[1,768,3,384]{3,1,2,0:T(8,128)(2,1)}) %all-gather.39.cloned.1.call-update) | async-done | bytes 1769488 | tf_op jit(solution)/shard_map/all_gather | solution.py:84
  88.5 39.6 %all-gather.1 = bf16[1,384,768]{2,1,0:T(8,128)(2,1)} all-gather(bf16[1,24,768]{2,1,0:T(8,128)(2,1)S(1)} %get-tuple-element.207), channel_id=3, replica_groups=mesh['dp'=16,'mp'=2] {'dp'}, dimensions={1}, use_global_device_ids=true | all-gather | bytes 626688 | tf_op jit(solution)/shard_map/all_gather | solution.py:85
  198.3 32.1 %reduce-scatter.17.cloned.1.call-done = f32[384,768]{1,0:T(8,128)} async-done(((f32[768,768]{1,0:T(8,128)}), f32[384,768]{1,0:T(8,128)}) %reduce-scatter.17.cloned.1.call-update) | async-done | bytes 1179664 | tf_op jit(solution)/shard_map/reduce_scatter | solution.py:96
  235.6 39.8 %all-gather.41.cloned.1.call-done = bf16[1,768,1536]{2,1,0:T(8,128)(2,1)} async-done(((bf16[1,48,1536]{2,1,0:T(8,128)(2,1)}), bf16[1,768,1536]{2,1,0:T(8,128)(2,1)}) %all-gather.41.cloned.1.call-update) | async-done | bytes 2359312 | tf_op jit(solution)/shard_map/all_gather | solution.py:86
  275.4 23.5 %all-gather.25.cloned.1.call-done = bf16[768,768]{1,0:T(8,128)(2,1)} async-done(((bf16[384,768]{1,0:T(8,128)(2,1)}), bf16[768,768]{1,0:T(8,128)(2,1)}) %all-gather.25.cloned.1.call-update) | async-done | bytes 1179664 | tf_op jit(solution)/shard_map/all_gather | solution.py:92
  305.9 38.0 %all-gather.43.cloned.1.call-done = bf16[1,1536,768]{2,1,0:T(8,128)(2,1)} async-done(((bf16[1,96,768]{2,1,0:T(8,128)(2,1)}), bf16[1,1536,768]{2,1,0:T(8,128)(2,1)}) %all-gather.43.cloned.1.call-update) | async-done | bytes 2359312 | tf_op jit(solution)/shard_map/all_gather | solution.py:87
  350.5 32.9 %reduce-scatter.19.cloned.1.call-done = f32[384,768]{1,0:T(8,128)} async-done(((f32[768,768]{1,0:T(8,128)}), f32[384,768]{1,0:T(8,128)}) %reduce-scatter.19.cloned.1.call-update) | async-done | bytes 1179664 | tf_op jit(solution)/shard_map/reduce_scatter | solution.py:96
  387.1 39.1 %all-gather.45.cloned.1.call-done = bf16[1,768,3,384]{3,1,2,0:T(8,128)(2,1)} async-done(((bf16[1,48,3,384]{3,1,2,0:T(8,128)(2,1)}), bf16[1,768,3,384]{3,1,2,0:T(8,128)(2,1)}) %all-gather.45.cloned.1.call-update) | async-done | bytes 1769488 | tf_op jit(solution)/shard_map/all_gather | solution.py:84
  428.8 21.0 %all-gather.27.cloned.1.call-done = bf16[768,768]{1,0:T(8,128)(2,1)} async-done(((bf16[384,768]{1,0:T(8,128)(2,1)}), bf16[768,768]{1,0:T(8,128)(2,1)}) %all-gather.27.cloned.1.call-update) | async-done | bytes 1179664 | tf_op jit(solution)/shard_map/all_gather | solution.py:92
  457.2 39.2 %all-gather.5 = bf16[1,384,768]{2,1,0:T(8,128)(2,1)S(1)} all-gather(bf16[1,24,768]{2,1,0:T(8,128)(2,1)S(1)} %copy-done.50), channel_id=7, replica_groups=mesh['dp'=16,'mp'=2] {'dp'}, dimensions={1}, use_global_device_ids=true | all-gather | bytes 626688 | tf_op jit(solution)/shard_map/all_gather | solution.py:85
  557.9 33.6 %reduce-scatter.21.cloned.1.call-done = f32[384,768]{1,0:T(8,128)} async-done(((f32[768,768]{1,0:T(8,128)}), f32[384,768]{1,0:T(8,128)}) %reduce-scatter.21.cloned.1.call-update) | async-done | bytes 1179664 | tf_op jit(solution)/shard_map/reduce_scatter | solution.py:96
  599.2 37.5 %all-gather.47.cloned.1.call-done = bf16[1,768,1536]{2,1,0:T(8,128)(2,1)} async-done(((bf16[1,48,1536]{2,1,0:T(8,128)(2,1)}), bf16[1,768,1536]{2,1,0:T(8,128)(2,1)}) %all-gather.47.cloned.1.call-update) | async-done | bytes 2359312 | tf_op jit(solution)/shard_map/all_gather | solution.py:86
  636.7 23.5 %all-gather.29.cloned.1.call-done = bf16[768,768]{1,0:T(8,128)(2,1)} async-done(((bf16[384,768]{1,0:T(8,128)(2,1)}), bf16[768,768]{1,0:T(8,128)(2,1)}) %all-gather.29.cloned.1.call-update) | async-done | bytes 1179664 | tf_op jit(solution)/shard_map/all_gather | solution.py:92
  685.1 44.5 %all-gather.49.cloned.1.call-done = bf16[1,1536,768]{2,1,0:T(8,128)(2,1)} async-done(((bf16[1,96,768]{2,1,0:T(8,128)(2,1)}), bf16[1,1536,768]{2,1,0:T(8,128)(2,1)}) %all-gather.49.cloned.1.call-update) | async-done | bytes 2359312 | tf_op jit(solution)/shard_map/all_gather | solution.py:87
  746.7 27.8 %reduce-scatter.25.cloned.1.call-done = f32[384,768]{1,0:T(8,128)} async-done(((f32[768,768]{1,0:T(8,128)}), f32[384,768]{1,0:T(8,128)}) %reduce-scatter.25.cloned.1.call-update) | async-done | bytes 1179664 | tf_op jit(solution)/shard_map/reduce_scatter | solution.py:96
  777.9 33.6 %reduce-scatter.23.cloned.1.call-done = f32[384,768]{1,0:T(8,128)} async-done(((f32[768,768]{1,0:T(8,128)}), f32[384,768]{1,0:T(8,128)}) %reduce-scatter.23.cloned.1.call-update) | async-done | bytes 1179664 | tf_op jit(solution)/shard_map/reduce_scatter | solution.py:96
  818.3 22.4 %all-gather.33.cloned.1.call-done = bf16[768,768]{1,0:T(8,128)(2,1)} async-done(((bf16[384,768]{1,0:T(8,128)(2,1)}), bf16[768,768]{1,0:T(8,128)(2,1)}) %all-gather.33.cloned.1.call-update) | async-done | bytes 1179664 | tf_op jit(solution)/shard_map/all_gather | solution.py:92
  862.5 28.0 %multiply_convert_fusion.1 = bf16[6,768,2304]{2,1,0:T(8,128)(2,1)} fusion(f32[6,768,2304]{2,1,0:T(8,128)} %get-tuple-element.219, bf16[768,6,64]{0,2,1:T(8,128)(2,1)S(1)} %bitcast.283, f32[6,768]{1,0:T(8,128)S(1)} %bitcast.293, f32[6,768]{1,0:T(8,128)S(1)} %copy-done.74, pred[768,2304]{1,0:T(8,128)(4,1)S(1)} %fusion.7, ...), kind=kOutput, calls=%fused_computation.1 | convolution fusion | flops 1422655488 | bytes 67866624 | tf_op jit(solution)/shard_map/while/body/eval_jaxpr/qhd,khd->hqk/dot_general | solution.py:148
  941.3 41.2 %reduce-scatter.27.cloned.1.call-done = f32[384,768]{1,0:T(8,128)} async-done(((f32[768,768]{1,0:T(8,128)}), f32[384,768]{1,0:T(8,128)}) %reduce-scatter.27.cloned.1.call-update) | async-done | bytes 1179664 | tf_op jit(solution)/shard_map/reduce_scatter | solution.py:96
  988.1 22.9 %all-gather.35.cloned.1.call-done = bf16[768,768]{1,0:T(8,128)(2,1)} async-done(((bf16[384,768]{1,0:T(8,128)(2,1)}), bf16[768,768]{1,0:T(8,128)(2,1)}) %all-gather.35.cloned.1.call-update) | async-done | bytes 1179664 | tf_op jit(solution)/shard_map/all_gather | solution.py:92
  1022.2 34.9 %reduce-scatter.29.cloned.1.call-done = f32[384,768]{1,0:T(8,128)} async-done(((f32[768,768]{1,0:T(8,128)}), f32[384,768]{1,0:T(8,128)}) %reduce-scatter.29.cloned.1.call-update) | async-done | bytes 1179664 | tf_op jit(solution)/shard_map/reduce_scatter | solution.py:96
  1062.9 22.6 %all-gather.37.cloned.1.call-done = bf16[768,768]{1,0:T(8,128)(2,1)} async-done(((bf16[384,768]{1,0:T(8,128)(2,1)}), bf16[768,768]{1,0:T(8,128)(2,1)}) %all-gather.37.cloned.1.call-update) | async-done | bytes 1179664 | tf_op jit(solution)/shard_map/all_gather | solution.py:92
  1107.1 28.2 %multiply_convert_fusion = bf16[6,768,2304]{2,1,0:T(8,128)(2,1)} fusion(f32[6,768,2304]{2,1,0:T(8,128)} %get-tuple-element.215, bf16[768,6,64]{0,2,1:T(8,128)(2,1)S(1)} %bitcast.280, f32[6,768]{1,0:T(8,128)S(1)} %bitcast.292, f32[6,768]{1,0:T(8,128)S(1)} %copy-done.73, pred[768,2304]{1,0:T(8,128)(4,1)S(1)} %fusion.7, ...), kind=kOutput, calls=%fused_computation | convolution fusion | flops 1422655488 | bytes 67866624 | tf_op jit(solution)/shard_map/while/body/eval_jaxpr/qhd,khd->hqk/dot_general | solution.py:148
  1260.2 42.7 %reduce-scatter.47.cloned.1.call-done = f32[96,768]{1,0:T(8,128)} async-done(((f32[1536,768]{1,0:T(8,128)}), f32[96,768]{1,0:T(8,128)}) %reduce-scatter.47.cloned.1.call-update) | async-done | bytes 294928 | tf_op jit(solution)/shard_map/reduce_scatter | solution.py:340
  1302.9 78.5 %reduce-scatter.45.cloned.1.call-done = f32[96,768]{1,0:T(8,128)} async-done(((f32[1536,768]{1,0:T(8,128)}), f32[96,768]{1,0:T(8,128)}) %reduce-scatter.45.cloned.1.call-update) | async-done | bytes 294928 | tf_op jit(solution)/shard_map/reduce_scatter | solution.py:340
  1383.3 76.8 %reduce-scatter.43.cloned.1.call-done = f32[48,1536]{1,0:T(8,128)} async-done(((f32[768,1536]{1,0:T(8,128)}), f32[48,1536]{1,0:T(8,128)}) %reduce-scatter.43.cloned.1.call-update) | async-done | bytes 294928 | tf_op jit(solution)/shard_map/reduce_scatter | solution.py:339
  1460.1 78.5 %reduce-scatter.41.cloned.1.call-done = f32[48,1536]{1,0:T(8,128)} async-done(((f32[768,1536]{1,0:T(8,128)}), f32[48,1536]{1,0:T(8,128)}) %reduce-scatter.41.cloned.1.call-update) | async-done | bytes 294928 | tf_op jit(solution)/shard_map/reduce_scatter | solution.py:339
  1540.5 59.0 %reduce-scatter.39.cloned.1.call-done = f32[24,768]{1,0:T(8,128)} async-done(((f32[384,768]{1,0:T(8,128)}), f32[24,768]{1,0:T(8,128)}) %reduce-scatter.39.cloned.1.call-update) | async-done | bytes 73744 | tf_op jit(solution)/shard_map/reduce_scatter | solution.py:338
  1599.5 60.9 %reduce-scatter.37.cloned.1.call-done = f32[24,768]{1,0:T(8,128)} async-done(((f32[384,768]{1,0:T(8,128)}), f32[24,768]{1,0:T(8,128)}) %reduce-scatter.37.cloned.1.call-update) | async-done | bytes 73744 | tf_op jit(solution)/shard_map/reduce_scatter | solution.py:338
  1664.7 128.0 %all-reduce.3.cloned.1.call-done = (f32[1,2,768]{2,1,0:T(2,128)}, f32[1,2,768]{2,1,0:T(2,128)}, f32[1,3072]{1,0:T(1,128)}, f32[1,3072]{1,0:T(1,128)}, f32[1,2,76...) async-done(((f32[1,2,768]{2,1,0:T(2,128)}, f32[1,2,768]{2,1,0:T(2,128)}, ...) | async-done | bytes 73744 | tf_op jit(solution)/shard_map/psum | solution.py:342
  1799.2 68.4 %reduce-scatter.35.cloned.1.call-done = f32[48,3,384]{2,0,1:T(8,128)} async-done(((f32[768,3,384]{2,0,1:T(8,128)}), f32[48,3,384]{2,0,1:T(8,128)}) %reduce-scatter.35.cloned.1.call-update) | async-done | bytes 221200 | tf_op jit(solution)/shard_map/reduce_scatter | solution.py:337
  1867.6 70.9 %reduce-scatter.33.cloned.1.call-done = f32[48,3,384]{2,0,1:T(8,128)} async-done(((f32[768,3,384]{2,0,1:T(8,128)}), f32[48,3,384]{2,0,1:T(8,128)}) %reduce-scatter.33.cloned.1.call-update) | async-done | bytes 221200 | tf_op jit(solution)/shard_map/reduce_scatter | solution.py:337
  (444 shorter events, 523.2 us)
Async XLA Ops:
  9.0 68.7 %all-gather.23.cloned.1.call-start = ((), (), s32[]{:S(2)}) async-start(), calls=%async_computation.16 | async-start | bytes 1769472 | tf_op jit(solution)/shard_map/all_gather | solution.py:92
  13.4 217.0 %reduce-scatter.17.cloned.1.call-start = ((), (), s32[]{:S(2)}) async-start(), calls=%async_computation.17 | async-start | bytes 3538944 | tf_op jit(solution)/shard_map/reduce_scatter | solution.py:96
  82.9 49.3 %collective-permute-start.1 = (bf16[768,768]{0,1:T(8,128)(2,1)}, bf16[768,768]{0,1:T(8,128)(2,1)}, u32[]{:S(2)}, u32[]{:S(2)}) collective-permute-start(bf16[768,768]{0,1:T(8,128)(2,1)} %bitcast.6), channel_id=1, source_target_pairs={{2,0},{4,2},{6,4},{8,6},{10,8},{12,10},{14,12},{16,14},{18,16},{20... | collective-permute-start | bytes 3538952 | tf_op jit(solution)/shard_map/ppermute | solution.py:18
  84.2 48.0 %collective-permute-start = (bf16[768,768]{0,1:T(8,128)(2,1)}, bf16[768,768]{0,1:T(8,128)(2,1)}, u32[]{:S(2)}, u32[]{:S(2)}) collective-permute-start(bf16[768,768]{0,1:T(8,128)(2,1)} %bitcast.6), channel_id=1, source_target_pairs={{0,2},{2,4},{4,6},{6,8},{8,10},{10,12},{12,14},{14,16},{16,18},{18... | collective-permute-start | bytes 3538952 | tf_op jit(solution)/shard_map/ppermute | solution.py:15
  195.9 79.5 %all-gather.41.cloned.1.call-start = ((), (), s32[]{:S(2)}) async-start(), calls=%async_computation.41 | async-start | bytes 2506752 | tf_op jit(solution)/shard_map/all_gather | solution.py:86
  197.6 101.3 %all-gather.25.cloned.1.call-start = ((), (), s32[]{:S(2)}) async-start(), calls=%async_computation.18 | async-start | bytes 1769472 | tf_op jit(solution)/shard_map/all_gather | solution.py:92
  234.0 110.0 %all-gather.43.cloned.1.call-start = ((), (), s32[]{:S(2)}) async-start(), calls=%async_computation.42 | async-start | bytes 2506752 | tf_op jit(solution)/shard_map/all_gather | solution.py:87
  234.8 148.6 %reduce-scatter.19.cloned.1.call-start = ((), (), s32[]{:S(2)}) async-start(), calls=%async_computation.19 | async-start | bytes 3538944 | tf_op jit(solution)/shard_map/reduce_scatter | solution.py:96
  349.8 76.5 %all-gather.45.cloned.1.call-start = ((), (), s32[]{:S(2)}) async-start(), calls=%async_computation.43 | async-start | bytes 1880064 | tf_op jit(solution)/shard_map/all_gather | solution.py:84
  350.5 99.3 %all-gather.27.cloned.1.call-start = ((), (), s32[]{:S(2)}) async-start(), calls=%async_computation.20 | async-start | bytes 1769472 | tf_op jit(solution)/shard_map/all_gather | solution.py:92
  387.0 204.5 %reduce-scatter.21.cloned.1.call-start = ((), (), s32[]{:S(2)}) async-start(), calls=%async_computation.21 | async-start | bytes 3538944 | tf_op jit(solution)/shard_map/reduce_scatter | solution.py:96
  557.1 79.6 %all-gather.47.cloned.1.call-start = ((), (), s32[]{:S(2)}) async-start(), calls=%async_computation.44 | async-start | bytes 2506752 | tf_op jit(solution)/shard_map/all_gather | solution.py:86
  557.8 102.4 %all-gather.29.cloned.1.call-start = ((), (), s32[]{:S(2)}) async-start(), calls=%async_computation.22 | async-start | bytes 1769472 | tf_op jit(solution)/shard_map/all_gather | solution.py:92
  595.1 90.0 %all-gather.31.cloned.1.call-start = ((), (), s32[]{:S(2)}) async-start(), calls=%async_computation.24 | async-start | bytes 1769472 | tf_op jit(solution)/shard_map/all_gather | solution.py:92
  598.4 131.2 %all-gather.49.cloned.1.call-start = ((), (), s32[]{:S(2)}) async-start(), calls=%async_computation.45 | async-start | bytes 2506752 | tf_op jit(solution)/shard_map/all_gather | solution.py:87
  598.9 175.6 %reduce-scatter.25.cloned.1.call-start = ((), (), s32[]{:S(2)}) async-start(), calls=%async_computation.25 | async-start | bytes 3538944 | tf_op jit(solution)/shard_map/reduce_scatter | solution.py:96
  740.8 70.6 %reduce-scatter.23.cloned.1.call-start = ((), (), s32[]{:S(2)}) async-start(), calls=%async_computation.23 | async-start | bytes 3538944 | tf_op jit(solution)/shard_map/reduce_scatter | solution.py:96
  746.7 94.0 %all-gather.33.cloned.1.call-start = ((), (), s32[]{:S(2)}) async-start(), calls=%async_computation.26 | async-start | bytes 1769472 | tf_op jit(solution)/shard_map/all_gather | solution.py:92
  817.8 164.6 %reduce-scatter.27.cloned.1.call-start = ((), (), s32[]{:S(2)}) async-start(), calls=%async_computation.27 | async-start | bytes 3538944 | tf_op jit(solution)/shard_map/reduce_scatter | solution.py:96
  941.2 69.7 %all-gather.35.cloned.1.call-start = ((), (), s32[]{:S(2)}) async-start(), calls=%async_computation.28 | async-start | bytes 1769472 | tf_op jit(solution)/shard_map/all_gather | solution.py:92
  988.0 69.0 %reduce-scatter.29.cloned.1.call-start = ((), (), s32[]{:S(2)}) async-start(), calls=%async_computation.29 | async-start | bytes 3538944 | tf_op jit(solution)/shard_map/reduce_scatter | solution.py:96
  1022.2 63.4 %all-gather.37.cloned.1.call-start = ((), (), s32[]{:S(2)}) async-start(), calls=%async_computation.30 | async-start | bytes 1769472 | tf_op jit(solution)/shard_map/all_gather | solution.py:92
  1062.7 179.0 %reduce-scatter.31.cloned.1.call-start = ((), (), s32[]{:S(2)}) async-start(), calls=%async_computation.31 | async-start | bytes 3538944 | tf_op jit(solution)/shard_map/reduce_scatter | solution.py:96
  1182.4 120.5 %reduce-scatter.47.cloned.1.call-start = ((), (), s32[]{:S(2)}) async-start(), calls=%async_computation.39 | async-start | bytes 5013504 | tf_op jit(solution)/shard_map/reduce_scatter | solution.py:340
  1189.5 191.9 %reduce-scatter.45.cloned.1.call-start = ((), (), s32[]{:S(2)}) async-start(), calls=%async_computation.38 | async-start | bytes 5013504 | tf_op jit(solution)/shard_map/reduce_scatter | solution.py:340
  1196.7 263.4 %reduce-scatter.43.cloned.1.call-start = ((), (), s32[]{:S(2)}) async-start(), calls=%async_computation.37 | async-start | bytes 5013504 | tf_op jit(solution)/shard_map/reduce_scatter | solution.py:339
  1203.9 334.7 %reduce-scatter.41.cloned.1.call-start = ((), (), s32[]{:S(2)}) async-start(), calls=%async_computation.36 | async-start | bytes 5013504 | tf_op jit(solution)/shard_map/reduce_scatter | solution.py:339
  1211.0 388.5 %reduce-scatter.39.cloned.1.call-start = ((), (), s32[]{:S(2)}) async-start(), calls=%async_computation.35 | async-start | bytes 1253376 | tf_op jit(solution)/shard_map/reduce_scatter | solution.py:338
  1214.1 446.2 %reduce-scatter.37.cloned.1.call-start = ((), (), s32[]{:S(2)}) async-start(), calls=%async_computation.34 | async-start | bytes 1253376 | tf_op jit(solution)/shard_map/reduce_scatter | solution.py:338
  1217.8 574.8 %all-reduce.3.cloned.1.call-start = ((), (), s32[]{:S(2)}) async-start(), calls=%async_computation.46 | async-start | bytes 147456 | tf_op jit(solution)/shard_map/psum | solution.py:342
  1246.0 621.6 %reduce-scatter.35.cloned.1.call-start = ((), (), s32[]{:S(2)}) async-start(), calls=%async_computation.33 | async-start | bytes 3760128 | tf_op jit(solution)/shard_map/reduce_scatter | solution.py:337
  1251.0 687.5 %reduce-scatter.33.cloned.1.call-start = ((), (), s32[]{:S(2)}) async-start(), calls=%async_computation.32 | async-start | bytes 3760128 | tf_op jit(solution)/shard_map/reduce_scatter | solution.py:337
  (104 other events, 3123.2 us)
Sparse Core Ops, SparseCore 0:
  10.9 43.1 all-gather.38
  56.2 21.4 all-gather.22
  196.0 34.2 reduce-scatter.16
  233.1 42.2 all-gather.40
  277.4 21.4 all-gather.24
  301.6 42.2 all-gather.42
  349.9 33.5 reduce-scatter.18
  385.7 40.4 all-gather.44
  428.3 21.4 all-gather.26
  557.2 34.2 reduce-scatter.20
  594.4 42.2 all-gather.46
  638.7 21.4 all-gather.28
  662.3 22.7 all-gather.30
  687.2 42.2 all-gather.48
  741.0 33.5 reduce-scatter.24
  776.6 34.7 reduce-scatter.22
  817.9 22.7 all-gather.32
  941.4 41.0 reduce-scatter.26
  988.2 22.7 all-gather.34
  1022.3 34.7 reduce-scatter.28
  1062.8 22.7 all-gather.36
  1182.5 40.8 reduce-scatter.30
  1227.3 75.5 reduce-scatter.46
  1306.6 74.7 reduce-scatter.44
  1385.3 74.7 reduce-scatter.42
  1463.8 74.7 reduce-scatter.40
  1542.1 57.3 reduce-scatter.38
  1603.1 57.1 reduce-scatter.36
  1667.9 124.6 all-reduce.2
  1796.3 71.2 reduce-scatter.34
  1871.5 66.9 reduce-scatter.32
where the time goes:
time: 1950 us
  waiting for transfers between devices  1310 us (67%)
  matrix products  312 us (16%)
  other arithmetic  129 us (7%)
  blocking collectives  78.8 us (4%)
  local copies, waits for them, and re-layouts  73.5 us (4%)
  starting transfers between devices  23.5 us (1%)
    reduce_scatter x8, waiting for transfers between devices, sum_rows(): lax.psum_scatter(jnp.dot(left, right, preferred_element_type=jnp.float32)...  236 us
    all_gather x8, waiting for transfers between devices, gather_rows(): return lax.all_gather(values, 'mp', axis=0, tiled=True)  175 us
    reduce_scatter x2, waiting for transfers between devices, body(): lax.psum_scatter(mats_grad[2], 'dp', scatter_dimension=0, tiled=True)  155 us
    reduce_scatter x2, waiting for transfers between devices, body(): lax.psum_scatter(mats_grad[0], 'dp', scatter_dimension=0, tiled=True)  139 us
    psum x1, waiting for transfers between devices, body(): lax.psum((small[0], small[1], small[2], small[3], small[4]), ('dp', 'mp'))  128 us
    reduce_scatter x2, waiting for transfers between devices, body(): lax.psum_scatter(mats_grad[3], 'dp', scatter_dimension=0, tiled=True)  121 us
    reduce_scatter x2, waiting for transfers between devices, body(): lax.psum_scatter(mats_grad[1], 'dp', scatter_dimension=0, tiled=True)  120 us
    all_gather x2, waiting for transfers between devices, fetch_weights(): lax.all_gather(down_weight[depth], 'dp', axis=0, tiled=True)  82.5 us
  transfers between devices with their start and end apart: 39, of which 30 were waited for; matrix products, arithmetic and copies ran while one was open for 9% of the time, Pallas kernels for 0%

commit v1 on v0

--- a/solution.py
+++ b/solution.py
@@ -5,6 +5,19 @@
 
 HD = 64
 epsilon = 1e-05
+
+
+def ring_gather(shard, axis, dim):
+    size, index, rows = (lax.axis_size(axis), lax.axis_index(axis), shard.shape[dim])
+    right = [(i, (i + 1) % size) for i in range(size)]
+    out = jnp.zeros((*shard.shape[:dim], size * rows, *shard.shape[dim + 1 :]), shard.dtype)
+    held = shard
+    for step in range(size):
+        source = (index - step) % size
+        out = lax.dynamic_update_slice_in_dim(out, held, source * rows, axis=dim)
+        if step < size - 1:
+            held = lax.ppermute(held, axis, right)
+    return out
 
 
 def padded_2(block, sides, width):
@@ -83,7 +96,7 @@
     return (
         lax.all_gather(qkv_weight[depth], "dp", axis=0, tiled=True),
         lax.all_gather(proj_weight[depth], "dp", axis=0, tiled=True),
-        lax.all_gather(up_weight[depth], "dp", axis=0, tiled=True),
+        ring_gather(up_weight[depth], "dp", 0),
         lax.all_gather(down_weight[depth], "dp", axis=0, tiled=True),
     )
 

time: 1950 us -> 1960 us (level)
  local copies, waits for them, and re-layouts: 73.5 us -> 107 us
  waiting for transfers between devices: 1310 us -> 1290 us
    ppermute x0 -> x30, waiting for transfers between devices: none -> 200 us  [ring_gather(): held = lax.ppermute(held, axis, right)]
    all_gather x2, waiting for transfers between devices: 82.5 us -> 0.01 us  [fetch_weights(): lax.all_gather(down_weight[depth], 'dp', axis=0, tiled=True)]
    all_gather x2 -> x0, waiting for transfers between devices: 77.2 us -> none  [fetch_weights(): lax.all_gather(up_weight[depth], 'dp', axis=0, tiled=True)]
    all_gather x8, waiting for transfers between devices: 175 us -> 110 us  [gather_rows(): return lax.all_gather(values, 'mp', axis=0, tiled=True)]
    dynamic_update_slice x0 -> x32, local copies, waits for them, and re-layouts: none -> 22.4 us  [ring_gather(): out = lax.dynamic_update_slice_in_dim(out, held, source * rows, axis=dim)]
  transfers between devices with their start and end apart: 39 -> 67, of which waited for: 30 -> 53; matrix products, arithmetic and copies ran while one was open for 9% -> 10% of each run, Pallas kernels for 0% -> 0%
where the time goes in v1:
time: 1960 us; the launch traced here: 1950 us
  waiting for transfers between devices  1290 us (66%)
  matrix products  311 us (16%)
  other arithmetic  125 us (6%)
  local copies, waits for them, and re-layouts  107 us (5%)
  blocking collectives  80.2 us (4%)
  starting transfers between devices  23.6 us (1%)
    reduce_scatter x8, waiting for transfers between devices, sum_rows(): lax.psum_scatter(jnp.dot(left, right, preferred_element_type=jnp.float32)...  234 us
    ppermute x30, waiting for transfers between devices, ring_gather(): held = lax.ppermute(held, axis, right)  200 us
    reduce_scatter x2, waiting for transfers between devices, body(): lax.psum_scatter(mats_grad[2], 'dp', scatter_dimension=0, tiled=True)  155 us
    reduce_scatter x2, waiting for transfers between devices, body(): lax.psum_scatter(mats_grad[0], 'dp', scatter_dimension=0, tiled=True)  139 us
    psum x1, waiting for transfers between devices, body(): lax.psum((small[0], small[1], small[2], small[3], small[4]), ('dp', 'mp'))  128 us
    reduce_scatter x2, waiting for transfers between devices, body(): lax.psum_scatter(mats_grad[3], 'dp', scatter_dimension=0, tiled=True)  123 us
    reduce_scatter x2, waiting for transfers between devices, body(): lax.psum_scatter(mats_grad[1], 'dp', scatter_dimension=0, tiled=True)  120 us
    all_gather x8, waiting for transfers between devices, gather_rows(): return lax.all_gather(values, 'mp', axis=0, tiled=True)  110 us
  transfers between devices with their start and end apart: 67, of which 53 were waited for; matrix products, arithmetic and copies ran while one was open for 10% of the time, Pallas kernels for 0%

profile of v1, /device:TPU:0, one launch (start us, length us, event | category | flops | bytes accessed | tf_op | source)
XLA Modules:
  0.0 1953.2 jit_solution(7616251466650162325)
XLA Ops:
  15.6 38.5 %all-gather.35.cloned.1.call-done = bf16[1,768,3,384]{3,1,2,0:T(8,128)(2,1)} async-done(((bf16[1,48,3,384]{3,1,2,0:T(8,128)(2,1)}), bf16[1,768,3,384]{3,1,2,0:T(8,128)(2,1)}) %all-gather.35.cloned.1.call-update) | async-done | bytes 1769488 | tf_op jit(solution)/shard_map/all_gather | solution.py:97
  56.7 21.0 %all-gather.19.cloned.1.call-done = bf16[768,768]{1,0:T(8,128)(2,1)} async-done(((bf16[384,768]{1,0:T(8,128)(2,1)}), bf16[768,768]{1,0:T(8,128)(2,1)}) %all-gather.19.cloned.1.call-update) | async-done | bytes 1179664 | tf_op jit(solution)/shard_map/all_gather | solution.py:105
  88.5 39.6 %all-gather.1 = bf16[1,384,768]{2,1,0:T(8,128)(2,1)} all-gather(bf16[1,24,768]{2,1,0:T(8,128)(2,1)S(1)} %get-tuple-element.207), channel_id=3, replica_groups=mesh['dp'=16,'mp'=2] {'dp'}, dimensions={1}, use_global_device_ids=true | all-gather | bytes 626688 | tf_op jit(solution)/shard_map/all_gather | solution.py:98
  153.9 20.7 %exponential_reduce_fusion.1 = f32[6,768]{1,0:T(8,128)S(1)} fusion(f32[6,768,2304]{2,1,0:T(8,128)} %get-tuple-element.215, f32[6,768]{1,0:T(8,128)} %get-tuple-element.214, pred[768,2304]{1,0:T(8,128)(4,1)S(1)} %fusion.7), kind=kLoop, calls=%fused_computation.6 | loop fusion | flops 42462720 | bytes 44273664 | tf_op jit(solution)/shard_map/while/body/eval_jaxpr/reduce_sum | solution.py:137
  197.5 33.0 %reduce-scatter.17.cloned.1.call-done = f32[384,768]{1,0:T(8,128)} async-done(((f32[768,768]{1,0:T(8,128)}), f32[384,768]{1,0:T(8,128)}) %reduce-scatter.17.cloned.1.call-update) | async-done | bytes 1179664 | tf_op jit(solution)/shard_map/reduce_scatter | solution.py:109
  362.7 31.1 %reduce-scatter.19.cloned.1.call-done = f32[384,768]{1,0:T(8,128)} async-done(((f32[768,768]{1,0:T(8,128)}), f32[384,768]{1,0:T(8,128)}) %reduce-scatter.19.cloned.1.call-update) | async-done | bytes 1179664 | tf_op jit(solution)/shard_map/reduce_scatter | solution.py:109
  397.5 39.1 %all-gather.39.cloned.1.call-done = bf16[1,768,3,384]{3,1,2,0:T(8,128)(2,1)} async-done(((bf16[1,48,3,384]{3,1,2,0:T(8,128)(2,1)}), bf16[1,768,3,384]{3,1,2,0:T(8,128)(2,1)}) %all-gather.39.cloned.1.call-update) | async-done | bytes 1769488 | tf_op jit(solution)/shard_map/all_gather | solution.py:97
  439.2 21.0 %all-gather.23.cloned.1.call-done = bf16[768,768]{1,0:T(8,128)(2,1)} async-done(((bf16[384,768]{1,0:T(8,128)(2,1)}), bf16[768,768]{1,0:T(8,128)(2,1)}) %all-gather.23.cloned.1.call-update) | async-done | bytes 1179664 | tf_op jit(solution)/shard_map/all_gather | solution.py:105
  467.6 40.6 %all-gather.4 = bf16[1,384,768]{2,1,0:T(8,128)(2,1)} all-gather(bf16[1,24,768]{2,1,0:T(8,128)(2,1)S(1)} %copy-done.56), channel_id=6, replica_groups=mesh['dp'=16,'mp'=2] {'dp'}, dimensions={1}, use_global_device_ids=true | all-gather | bytes 626688 | tf_op jit(solution)/shard_map/all_gather | solution.py:98
  527.8 19.9 %exponential_reduce_fusion = f32[6,768]{1,0:T(8,128)S(1)} fusion(f32[6,768,2304]{2,1,0:T(8,128)} %get-tuple-element.219, f32[6,768]{1,0:T(8,128)S(1)} %get-tuple-element.218, pred[768,2304]{1,0:T(8,128)(4,1)S(1)} %fusion.7), kind=kLoop, calls=%fused_computation.3 | loop fusion | flops 42462720 | bytes 44273664 | tf_op jit(solution)/shard_map/while/body/eval_jaxpr/reduce_sum | solution.py:137
  547.7 18.2 fusion.50
  569.5 34.4 %reduce-scatter.21.cloned.1.call-done = f32[384,768]{1,0:T(8,128)} async-done(((f32[768,768]{1,0:T(8,128)}), f32[384,768]{1,0:T(8,128)}) %reduce-scatter.21.cloned.1.call-update) | async-done | bytes 1179664 | tf_op jit(solution)/shard_map/reduce_scatter | solution.py:109
  750.8 26.2 %reduce-scatter.25.cloned.1.call-done = f32[384,768]{1,0:T(8,128)} async-done(((f32[768,768]{1,0:T(8,128)}), f32[384,768]{1,0:T(8,128)}) %reduce-scatter.25.cloned.1.call-update) | async-done | bytes 1179664 | tf_op jit(solution)/shard_map/reduce_scatter | solution.py:109
  780.3 33.6 %reduce-scatter.23.cloned.1.call-done = f32[384,768]{1,0:T(8,128)} async-done(((f32[768,768]{1,0:T(8,128)}), f32[384,768]{1,0:T(8,128)}) %reduce-scatter.23.cloned.1.call-update) | async-done | bytes 1179664 | tf_op jit(solution)/shard_map/reduce_scatter | solution.py:109
  820.6 22.7 %all-gather.29.cloned.1.call-done = bf16[768,768]{1,0:T(8,128)(2,1)} async-done(((bf16[384,768]{1,0:T(8,128)(2,1)}), bf16[768,768]{1,0:T(8,128)(2,1)}) %all-gather.29.cloned.1.call-update) | async-done | bytes 1179664 | tf_op jit(solution)/shard_map/all_gather | solution.py:105
  845.6 19.4 convolution_bitcast_fusion.1
  865.0 28.1 %multiply_convert_fusion.1 = bf16[6,768,2304]{2,1,0:T(8,128)(2,1)} fusion(f32[6,768,2304]{2,1,0:T(8,128)} %get-tuple-element.219, bf16[768,6,64]{0,2,1:T(8,128)(2,1)S(1)} %bitcast.281, f32[6,768]{1,0:T(8,128)S(1)} %bitcast.291, f32[6,768]{1,0:T(8,128)S(1)} %copy-done.82, pred[768,2304]{1,0:T(8,128)(4,1)S(1)} %fusion.7, ...), kind=kOutput, calls=%fused_computation.1 | convolution fusion | flops 1422655488 | bytes 67866624 | tf_op jit(solution)/shard_map/while/body/eval_jaxpr/qhd,khd->hqk/dot_general | solution.py:161
  944.1 40.9 %reduce-scatter.27.cloned.1.call-done = f32[384,768]{1,0:T(8,128)} async-done(((f32[768,768]{1,0:T(8,128)}), f32[384,768]{1,0:T(8,128)}) %reduce-scatter.27.cloned.1.call-update) | async-done | bytes 1179664 | tf_op jit(solution)/shard_map/reduce_scatter | solution.py:109
  990.7 22.9 %all-gather.31.cloned.1.call-done = bf16[768,768]{1,0:T(8,128)(2,1)} async-done(((bf16[384,768]{1,0:T(8,128)(2,1)}), bf16[768,768]{1,0:T(8,128)(2,1)}) %all-gather.31.cloned.1.call-update) | async-done | bytes 1179664 | tf_op jit(solution)/shard_map/all_gather | solution.py:105
  1026.3 34.9 %reduce-scatter.29.cloned.1.call-done = f32[384,768]{1,0:T(8,128)} async-done(((f32[768,768]{1,0:T(8,128)}), f32[384,768]{1,0:T(8,128)}) %reduce-scatter.29.cloned.1.call-update) | async-done | bytes 1179664 | tf_op jit(solution)/shard_map/reduce_scatter | solution.py:109
  1067.0 22.7 %all-gather.33.cloned.1.call-done = bf16[768,768]{1,0:T(8,128)(2,1)} async-done(((bf16[384,768]{1,0:T(8,128)(2,1)}), bf16[768,768]{1,0:T(8,128)(2,1)}) %all-gather.33.cloned.1.call-update) | async-done | bytes 1179664 | tf_op jit(solution)/shard_map/all_gather | solution.py:105
  1091.8 19.4 convolution_bitcast_fusion
  1111.2 28.1 %multiply_convert_fusion = bf16[6,768,2304]{2,1,0:T(8,128)(2,1)} fusion(f32[6,768,2304]{2,1,0:T(8,128)} %get-tuple-element.215, bf16[768,6,64]{0,2,1:T(8,128)(2,1)S(1)} %bitcast.278, f32[6,768]{1,0:T(8,128)S(1)} %bitcast.290, f32[6,768]{1,0:T(8,128)S(1)} %copy-done.80, pred[768,2304]{1,0:T(8,128)(4,1)S(1)} %fusion.7, ...), kind=kOutput, calls=%fused_computation | convolution fusion | flops 1422655488 | bytes 67866624 | tf_op jit(solution)/shard_map/while/body/eval_jaxpr/qhd,khd->hqk/dot_general | solution.py:161
  1264.5 44.5 %reduce-scatter.47.cloned.1.call-done = f32[96,768]{1,0:T(8,128)} async-done(((f32[1536,768]{1,0:T(8,128)}), f32[96,768]{1,0:T(8,128)}) %reduce-scatter.47.cloned.1.call-update) | async-done | bytes 294928 | tf_op jit(solution)/shard_map/reduce_scatter | solution.py:353
  1309.0 78.6 %reduce-scatter.45.cloned.1.call-done = f32[96,768]{1,0:T(8,128)} async-done(((f32[1536,768]{1,0:T(8,128)}), f32[96,768]{1,0:T(8,128)}) %reduce-scatter.45.cloned.1.call-update) | async-done | bytes 294928 | tf_op jit(solution)/shard_map/reduce_scatter | solution.py:353
  1389.5 76.8 %reduce-scatter.43.cloned.1.call-done = f32[48,1536]{1,0:T(8,128)} async-done(((f32[768,1536]{1,0:T(8,128)}), f32[48,1536]{1,0:T(8,128)}) %reduce-scatter.43.cloned.1.call-update) | async-done | bytes 294928 | tf_op jit(solution)/shard_map/reduce_scatter | solution.py:352
  1466.3 78.5 %reduce-scatter.41.cloned.1.call-done = f32[48,1536]{1,0:T(8,128)} async-done(((f32[768,1536]{1,0:T(8,128)}), f32[48,1536]{1,0:T(8,128)}) %reduce-scatter.41.cloned.1.call-update) | async-done | bytes 294928 | tf_op jit(solution)/shard_map/reduce_scatter | solution.py:352
  1546.7 59.1 %reduce-scatter.39.cloned.1.call-done = f32[24,768]{1,0:T(8,128)} async-done(((f32[384,768]{1,0:T(8,128)}), f32[24,768]{1,0:T(8,128)}) %reduce-scatter.39.cloned.1.call-update) | async-done | bytes 73744 | tf_op jit(solution)/shard_map/reduce_scatter | solution.py:351
  1605.8 60.7 %reduce-scatter.37.cloned.1.call-done = f32[24,768]{1,0:T(8,128)} async-done(((f32[384,768]{1,0:T(8,128)}), f32[24,768]{1,0:T(8,128)}) %reduce-scatter.37.cloned.1.call-update) | async-done | bytes 73744 | tf_op jit(solution)/shard_map/reduce_scatter | solution.py:351
  1670.2 128.3 %all-reduce.3.cloned.1.call-done = (f32[1,2,768]{2,1,0:T(2,128)}, f32[1,2,768]{2,1,0:T(2,128)}, f32[1,3072]{1,0:T(1,128)}, f32[1,3072]{1,0:T(1,128)}, f32[1,2,76...) async-done(((f32[1,2,768]{2,1,0:T(2,128)}, f32[1,2,768]{2,1,0:T(2,128)}, ...) | async-done | bytes 73744 | tf_op jit(solution)/shard_map/psum | solution.py:355
  1805.2 68.5 %reduce-scatter.35.cloned.1.call-done = f32[48,3,384]{2,0,1:T(8,128)} async-done(((f32[768,3,384]{2,0,1:T(8,128)}), f32[48,3,384]{2,0,1:T(8,128)}) %reduce-scatter.35.cloned.1.call-update) | async-done | bytes 221200 | tf_op jit(solution)/shard_map/reduce_scatter | solution.py:350
  1873.7 70.9 %reduce-scatter.33.cloned.1.call-done = f32[48,3,384]{2,0,1:T(8,128)} async-done(((f32[768,3,384]{2,0,1:T(8,128)}), f32[48,3,384]{2,0,1:T(8,128)}) %reduce-scatter.33.cloned.1.call-update) | async-done | bytes 221200 | tf_op jit(solution)/shard_map/reduce_scatter | solution.py:350
  (544 shorter events, 616.0 us)
Async XLA Ops:
  7.2 46.9 %all-gather.35.cloned.1.call-start = ((), (), s32[]{:S(2)}) async-start(), calls=%async_computation.40 | async-start | bytes 1880064 | tf_op jit(solution)/shard_map/all_gather | solution.py:97
  9.0 68.6 %all-gather.19.cloned.1.call-start = ((), (), s32[]{:S(2)}) async-start(), calls=%async_computation.16 | async-start | bytes 1769472 | tf_op jit(solution)/shard_map/all_gather | solution.py:105
  14.1 216.3 %reduce-scatter.17.cloned.1.call-start = ((), (), s32[]{:S(2)}) async-start(), calls=%async_computation.17 | async-start | bytes 3538944 | tf_op jit(solution)/shard_map/reduce_scatter | solution.py:109
  82.9 49.3 %collective-permute-start.1 = (bf16[768,768]{0,1:T(8,128)(2,1)}, bf16[768,768]{0,1:T(8,128)(2,1)}, u32[]{:S(2)}, u32[]{:S(2)}) collective-permute-start(bf16[768,768]{0,1:T(8,128)(2,1)} %bitcast.6), channel_id=1, source_target_pairs={{2,0},{4,2},{6,4},{8,6},{10,8},{12,10},{14,12},{16,14},{18,16},{20... | collective-permute-start | bytes 3538952 | tf_op jit(solution)/shard_map/ppermute | solution.py:31
  84.2 48.0 %collective-permute-start = (bf16[768,768]{0,1:T(8,128)(2,1)}, bf16[768,768]{0,1:T(8,128)(2,1)}, u32[]{:S(2)}, u32[]{:S(2)}) collective-permute-start(bf16[768,768]{0,1:T(8,128)(2,1)} %bitcast.6), channel_id=1, source_target_pairs={{0,2},{2,4},{4,6},{6,8},{8,10},{10,12},{12,14},{14,16},{16,18},{18... | collective-permute-start | bytes 3538952 | tf_op jit(solution)/shard_map/ppermute | solution.py:28
  196.0 153.1 %all-gather.21.cloned.1.call-start = ((), (), s32[]{:S(2)}) async-start(), calls=%async_computation.18 | async-start | bytes 1769472 | tf_op jit(solution)/shard_map/all_gather | solution.py:105
  234.1 122.1 %all-gather.37.cloned.1.call-start = ((), (), s32[]{:S(2)}) async-start(), calls=%async_computation.41 | async-start | bytes 2506752 | tf_op jit(solution)/shard_map/all_gather | solution.py:100
  235.6 158.2 %reduce-scatter.19.cloned.1.call-start = ((), (), s32[]{:S(2)}) async-start(), calls=%async_computation.19 | async-start | bytes 3538944 | tf_op jit(solution)/shard_map/reduce_scatter | solution.py:109
  361.9 74.7 %all-gather.39.cloned.1.call-start = ((), (), s32[]{:S(2)}) async-start(), calls=%async_computation.42 | async-start | bytes 1880064 | tf_op jit(solution)/shard_map/all_gather | solution.py:97
  362.7 97.5 %all-gather.23.cloned.1.call-start = ((), (), s32[]{:S(2)}) async-start(), calls=%async_computation.20 | async-start | bytes 1769472 | tf_op jit(solution)/shard_map/all_gather | solution.py:105
  397.4 206.5 %reduce-scatter.21.cloned.1.call-start = ((), (), s32[]{:S(2)}) async-start(), calls=%async_computation.21 | async-start | bytes 3538944 | tf_op jit(solution)/shard_map/reduce_scatter | solution.py:109
  463.1 45.1 %collective-permute-start.18 = (bf16[768,768]{0,1:T(8,128)(2,1)S(1)}, bf16[768,768]{0,1:T(8,128)(2,1)S(1)}, u32[]{:S(2)}, u32[]{:S(2)}) collective-permute-start(bf16[768,768]{0,1:T(8,128)(2,1)S(1)} %bitcast.265), channel_id=1, source_target_pairs={{2,0},{4,2},{6,4},{8,6},{10,8},{12,10},{14,12},{16,14},{18,16},{20... | collective-permute-start | bytes 3538952 | tf_op jit(solution)/shard_map/ppermute | solution.py:31
  569.4 155.7 %all-gather.25.cloned.1.call-start = ((), (), s32[]{:S(2)}) async-start(), calls=%async_computation.22 | async-start | bytes 1769472 | tf_op jit(solution)/shard_map/all_gather | solution.py:105
  607.5 124.6 %all-gather.27.cloned.1.call-start = ((), (), s32[]{:S(2)}) async-start(), calls=%async_computation.24 | async-start | bytes 1769472 | tf_op jit(solution)/shard_map/all_gather | solution.py:105
  610.8 121.3 %all-gather.41.cloned.1.call-start = ((), (), s32[]{:S(2)}) async-start(), calls=%async_computation.43 | async-start | bytes 2506752 | tf_op jit(solution)/shard_map/all_gather | solution.py:100
  611.4 165.6 %reduce-scatter.25.cloned.1.call-start = ((), (), s32[]{:S(2)}) async-start(), calls=%async_computation.25 | async-start | bytes 3538944 | tf_op jit(solution)/shard_map/reduce_scatter | solution.py:109
  744.9 69.0 %reduce-scatter.23.cloned.1.call-start = ((), (), s32[]{:S(2)}) async-start(), calls=%async_computation.23 | async-start | bytes 3538944 | tf_op jit(solution)/shard_map/reduce_scatter | solution.py:109
  750.8 92.5 %all-gather.29.cloned.1.call-start = ((), (), s32[]{:S(2)}) async-start(), calls=%async_computation.26 | async-start | bytes 1769472 | tf_op jit(solution)/shard_map/all_gather | solution.py:105
  820.3 164.7 %reduce-scatter.27.cloned.1.call-start = ((), (), s32[]{:S(2)}) async-start(), calls=%async_computation.27 | async-start | bytes 3538944 | tf_op jit(solution)/shard_map/reduce_scatter | solution.py:109
  944.1 69.4 %all-gather.31.cloned.1.call-start = ((), (), s32[]{:S(2)}) async-start(), calls=%async_computation.28 | async-start | bytes 1769472 | tf_op jit(solution)/shard_map/all_gather | solution.py:105
  990.6 70.6 %reduce-scatter.29.cloned.1.call-start = ((), (), s32[]{:S(2)}) async-start(), calls=%async_computation.29 | async-start | bytes 3538944 | tf_op jit(solution)/shard_map/reduce_scatter | solution.py:109
  1026.3 63.4 %all-gather.33.cloned.1.call-start = ((), (), s32[]{:S(2)}) async-start(), calls=%async_computation.30 | async-start | bytes 1769472 | tf_op jit(solution)/shard_map/all_gather | solution.py:105
  1066.7 178.8 %reduce-scatter.31.cloned.1.call-start = ((), (), s32[]{:S(2)}) async-start(), calls=%async_computation.31 | async-start | bytes 3538944 | tf_op jit(solution)/shard_map/reduce_scatter | solution.py:109
  1189.4 119.6 %reduce-scatter.47.cloned.1.call-start = ((), (), s32[]{:S(2)}) async-start(), calls=%async_computation.39 | async-start | bytes 5013504 | tf_op jit(solution)/shard_map/reduce_scatter | solution.py:353
  1194.9 192.7 %reduce-scatter.45.cloned.1.call-start = ((), (), s32[]{:S(2)}) async-start(), calls=%async_computation.38 | async-start | bytes 5013504 | tf_op jit(solution)/shard_map/reduce_scatter | solution.py:353
  1201.3 265.0 %reduce-scatter.43.cloned.1.call-start = ((), (), s32[]{:S(2)}) async-start(), calls=%async_computation.37 | async-start | bytes 5013504 | tf_op jit(solution)/shard_map/reduce_scatter | solution.py:352
  1207.6 337.2 %reduce-scatter.41.cloned.1.call-start = ((), (), s32[]{:S(2)}) async-start(), calls=%async_computation.36 | async-start | bytes 5013504 | tf_op jit(solution)/shard_map/reduce_scatter | solution.py:352
  1213.7 392.1 %reduce-scatter.39.cloned.1.call-start = ((), (), s32[]{:S(2)}) async-start(), calls=%async_computation.35 | async-start | bytes 1253376 | tf_op jit(solution)/shard_map/reduce_scatter | solution.py:351
  1216.9 449.6 %reduce-scatter.37.cloned.1.call-start = ((), (), s32[]{:S(2)}) async-start(), calls=%async_computation.34 | async-start | bytes 1253376 | tf_op jit(solution)/shard_map/reduce_scatter | solution.py:351
  1221.8 576.8 %all-reduce.3.cloned.1.call-start = ((), (), s32[]{:S(2)}) async-start(), calls=%async_computation.44 | async-start | bytes 147456 | tf_op jit(solution)/shard_map/psum | solution.py:355
  1249.3 624.4 %reduce-scatter.35.cloned.1.call-start = ((), (), s32[]{:S(2)}) async-start(), calls=%async_computation.33 | async-start | bytes 3760128 | tf_op jit(solution)/shard_map/reduce_scatter | solution.py:350
  1254.3 690.3 %reduce-scatter.33.cloned.1.call-start = ((), (), s32[]{:S(2)}) async-start(), calls=%async_computation.32 | async-start | bytes 3760128 | tf_op jit(solution)/shard_map/reduce_scatter | solution.py:350
  (138 other events, 3220.3 us)
Sparse Core Ops, SparseCore 0:
  10.9 43.1 all-gather.34
  56.2 21.4 all-gather.18
  196.1 34.2 reduce-scatter.16
  234.2 22.7 all-gather.20
  259.7 44.0 all-gather.36
  362.0 31.7 reduce-scatter.18
  396.1 40.4 all-gather.38
  438.7 21.4 all-gather.22
  569.6 34.2 reduce-scatter.20
  607.6 22.7 all-gather.24
  631.9 22.7 all-gather.26
  657.4 43.7 all-gather.40
  745.0 31.9 reduce-scatter.24
  779.1 34.7 reduce-scatter.22
  820.4 22.7 all-gather.28
  944.2 40.7 reduce-scatter.26
  990.7 22.7 all-gather.30
  1026.4 34.7 reduce-scatter.28
  1066.9 22.7 all-gather.32
  1189.6 39.9 reduce-scatter.30
  1233.4 75.5 reduce-scatter.46
  1312.9 74.6 reduce-scatter.44
  1391.5 74.7 reduce-scatter.42
  1470.0 74.7 reduce-scatter.40
  1548.4 57.3 reduce-scatter.38
  1609.3 57.1 reduce-scatter.36
  1673.9 124.5 all-reduce.2
  1802.4 71.2 reduce-scatter.34
  1877.6 66.9 reduce-scatter.32
